TPU v7x, 128 devices: a whole 4x4x4 slice. The times are simulated.
128 devices in a mesh: mem: 8 (over x, core), tile: 16 (over y, z).
Axes of the slice: x: 4, y: 4, z: 4, core: 2. Of those that a mesh axis runs over, the one named last changes fastest.
Arguments:
- control: float32 [16, 64, 320, 160], P('mem', None, 'tile'), may hold values from -6 to 6
- ens_perts: float32 [16, 2, 64, 320, 160], P('mem', None, None, 'tile'), may hold values from -8 to 8
- vert_corr: float32 [64, 64], replicated, may hold values from -0.75 to 0.75
- slab_wts: float32 [16, 4], replicated, may hold values from 0.25 to 2
- level_slab: int32 [64], replicated, may hold values from 0 to 15, as said below
Outputs:
- wind_share: float32 [2, 64, 320, 160], P(None, 'mem', 'tile')
- gradient: float32 [16, 64, 320, 160], P('mem', None, 'tile')
Inputs may be any that keep to these rules, and one draw needn't show every extreme that they name: `level_slab`: each slab holds a contiguous run of levels and slab numbers never fall with the level; every slab holds 1 to 8 levels, and one slab holds exactly 8.
All inputs are finite; a program needn't handle non-finite values.
Results may differ from a plain program's by a relative error of at most 0.0001.
Values sent between devices are 32-bit elements; how exact they have to be, the bound alone decides.
No kernel may reach another device: no remote copies, remote signals or barrier semaphores. Data moves between devices by JAX's collectives and lax.ppermute only.
A program may use at most 128 MiB of HBM per device.

v0:
```python
import math

import jax
import jax.numpy as jnp
import ml_dtypes
import numpy as np
from jax import lax
from jax.experimental import pallas as pl
from jax.experimental.pallas import tpu as pltpu
from jax.sharding import PartitionSpec as P


DILATIONS = (1, 2, 4, 8)
TILES = 16
MEMS = 8
ROWS = 20
NX = 320
NY = 160
LV = 64
MAIN = 128
TAIL = 32
GROUPS = ROWS // 4
K = ROWS + GROUPS
FULL = K // MEMS
Q = FULL + 1
LAST = K - 1
CUT = MAIN // MEMS
SHARE = FULL * LV + LV // MEMS
FIELDS = 8
NS = len(DILATIONS)
bf16 = jnp.bfloat16
f32 = jnp.float32


def line_filter(length, dilation):
    positions = np.arange(length)
    distance = np.abs(positions[None, :] - positions[:, None])
    inside = (distance % dilation == 0) & (distance <= 6 * dilation)
    ratio = (distance // dilation).astype(np.float64)
    kernel = np.where(inside, np.exp(-ratio * ratio / 8.0), 0.0)
    cubed = kernel @ kernel @ kernel
    centre = cubed[:, length // 2]
    return cubed / np.sqrt(np.sum(centre * centre))


def split_np(a):
    hi = a.astype(np.float32).astype(ml_dtypes.bfloat16)
    lo = (a - hi.astype(np.float64)).astype(np.float32).astype(ml_dtypes.bfloat16)
    return hi, lo


def x_order():
    order = []
    for j in range(4):
        for g in range(GROUPS):
            for t in range(TILES):
                order.append(ROWS * t + 4 * g + j)
    return np.array(order)


SPAN = TILES * GROUPS
FIRST = 2 * MAIN
REST = NX - FIRST
PAIR = REST + 2 * SPAN


def residue(j):
    return slice(SPAN * j, SPAN * (j + 1))


def constants():
    order = x_order()
    gx = [line_filter(NX, d)[order][:, order] for d in DILATIONS]
    gys = [line_filter(NY, d).T for d in DILATIONS]
    gy = np.concatenate([g[:, :MAIN] for g in gys] + [g[:, MAIN:] for g in gys], axis=1)
    high, low = split_np(gy)
    mains = NS * MAIN
    gy = np.concatenate([high, low[:, mains:], low[:, :mains]], axis=1)
    pairs, singles = [], []
    for p in range(2):
        rows = np.concatenate([np.arange(NX)[residue(p)], np.arange(NX)[residue(p + 2)]])
        pairs.append(np.concatenate([gx[0][rows, FIRST:], gx[1][rows][:, rows]], axis=1))
    for j in range(4):
        singles.append(np.concatenate([g[residue(j), residue(j)] for g in gx[2:]], axis=1))

    def stacked(a, axis):
        return jnp.asarray(np.concatenate(split_np(a), axis=axis))

    return (
        jnp.asarray(gy),
        stacked(gx[0][:, :FIRST], 0),
        stacked(np.stack(pairs), 1),
        stacked(np.stack(singles), 1),
    )


def split(a):
    hi = a.astype(bf16)
    lo = (a - hi.astype(f32)).astype(bf16)
    return hi, lo


def dot(a, b):
    return jnp.dot(a, b, preferred_element_type=f32)


def params(mib):
    return pltpu.CompilerParams(vmem_limit_bytes=mib * 1024 * 1024)


WHOLE = pl.BlockSpec(memory_space=pltpu.VMEM)
HBM = pl.BlockSpec(memory_space=pltpu.HBM)
SMEM = pl.BlockSpec(memory_space=pltpu.SMEM)
dma = pltpu.SemaphoreType.DMA


def in_hbm(x):
    return pltpu.with_memory_space_constraint(x, pltpu.HBM)


def main_at(r):
    return 5 * (r // 4) + r % 4


def tail_at(g):
    return 5 * g + 4


def own_cut(i, shape):
    return lax.broadcasted_iota(jnp.int32, shape, len(shape) - 1) // CUT == i


def pack_body(x_hbm, o_hbm, x_ref, o_ref, in_sems, out_sems):
    blocks = [(m, g) for m in range(x_ref.shape[0]) for g in range(GROUPS)]
    loads, stores = [], []
    for n, (m, g) in enumerate(blocks):
        rows = pl.ds(4 * g, 4)
        loads.append(pltpu.make_async_copy(x_hbm.at[m, rows], x_ref.at[m, rows], in_sems.at[n]))
        loads[-1].start()
    for n, (m, g) in enumerate(blocks):
        loads[n].wait()
        for j in range(4):
            o_ref[m, :, 5 * g + j] = x_ref[m, 4 * g + j, :, :MAIN].reshape(LV // 8, 8, MAIN)
        tails = [x_ref[m, 4 * g + j, :, MAIN:] for j in range(4)]
        o_ref[m, :, 5 * g + 4] = jnp.concatenate(tails, axis=1).reshape(LV // 8, 8, MAIN)
        part = (m, slice(None), pl.ds(5 * g, 5))
        stores.append(pltpu.make_async_copy(o_ref.at[part], o_hbm.at[part], out_sems.at[n]))
        stores[-1].start()
    for copy in stores:
        copy.wait()


def pack(x):
    n = x.shape[0]
    shape = (n, LV // 8, K, 8, MAIN)
    return pl.pallas_call(
        pack_body,
        in_specs=[HBM],
        out_specs=HBM,
        out_shape=pltpu.HBM(shape, f32),
        scratch_shapes=[
            pltpu.VMEM((n, ROWS, LV, NY), f32),
            pltpu.VMEM(shape, f32),
            dma((n * GROUPS,)),
            dma((n * GROUPS,)),
        ],
        compiler_params=params(12),
        name="pack",
    )(in_hbm(x))


def finish_body(y_hbm, c_ref, o_hbm, y_ref, o_ref, in_sems, sems):
    loads, stores = [], []
    for m in range(o_ref.shape[0]):
        for g in range(GROUPS):
            part = (m, slice(None), pl.ds(5 * g, 5))
            n = len(loads)
            loads.append(pltpu.make_async_copy(y_hbm.at[part], y_ref.at[part], in_sems.at[n]))
            loads[-1].start()
    for m in range(o_ref.shape[0]):
        for g in range(GROUPS):
            loads[len(stores)].wait()
            tails = y_ref[m, :, 5 * g + 4].reshape(LV, MAIN)
            for j in range(4):
                r = 4 * g + j
                main = y_ref[m, :, 5 * g + j].reshape(LV, MAIN)
                o_ref[m, r, :, :MAIN] = c_ref[m, r, :, :MAIN] + main
                tail = tails[:, TAIL * j : TAIL * (j + 1)]
                o_ref[m, r, :, MAIN:] = c_ref[m, r, :, MAIN:] + tail
            part = (m, pl.ds(4 * g, 4))
            n = len(stores)
            stores.append(pltpu.make_async_copy(o_ref.at[part], o_hbm.at[part], sems.at[n]))
            stores[-1].start()
    for copy in stores:
        copy.wait()


def finish(y, control):
    n = y.shape[0]
    shape = (n, ROWS, LV, NY)
    return pl.pallas_call(
        finish_body,
        in_specs=[HBM, WHOLE],
        out_specs=HBM,
        out_shape=pltpu.HBM(shape, f32),
        scratch_shapes=[
            pltpu.VMEM(y.shape, f32),
            pltpu.VMEM(shape, f32),
            dma((n * GROUPS,)),
            dma((n * GROUPS,)),
        ],
        compiler_params=params(16),
        name="finish",
    )(in_hbm(y), control)


def unpack_wind_body(me_ref, *refs):
    got_refs, o_ref, x_ref = refs[:MEMS], refs[MEMS], refs[MEMS + 1]
    for k in range(MEMS):
        x_ref[lax.rem(me_ref[0] + MEMS - k, MEMS)] = got_refs[k][...]
    for c in range(2):
        last = x_ref[0, c, FULL]
        for i in range(1, MEMS):
            last = jnp.where(own_cut(i, last.shape), x_ref[i, c, FULL], last)
        for r in range(ROWS):
            k = main_at(r)
            o_ref[c, r, :, :MAIN] = x_ref[k % MEMS, c, k // MEMS]
        for g in range(GROUPS):
            k = tail_at(g)
            tails = last if k == LAST else x_ref[k % MEMS, c, k // MEMS]
            for j in range(4):
                o_ref[c, 4 * g + j, :, MAIN:] = tails[:, TAIL * j : TAIL * (j + 1)]


def unpack_wind(me, got):
    return pl.pallas_call(
        unpack_wind_body,
        in_specs=[SMEM] + [WHOLE] * MEMS,
        out_shape=jax.ShapeDtypeStruct((2, ROWS, LV // MEMS, NY), f32),
        scratch_shapes=[pltpu.VMEM((MEMS, 2, Q, LV // MEMS, MAIN), f32)],
        compiler_params=params(8),
        name="unpack_wind",
    )(me, *got)


def spread_body(me_ref, x_hbm, *refs):
    o_refs, (x_ref, packed, in_sems, out_sems) = refs[:MEMS], refs[MEMS:]
    count = x_ref.shape[0]
    loads = [pltpu.make_async_copy(x_hbm.at[n], x_ref.at[n], in_sems.at[n]) for n in range(count)]
    for copy in loads:
        copy.start()
    stores = []
    for n in range(count):
        loads[n].wait()

        def keep(k, value):
            packed[n, k % MEMS, LV * (k // MEMS) : LV * (k // MEMS + 1)] = value

        for r in range(ROWS):
            keep(main_at(r), x_ref[n, r, :, :MAIN])
        for g in range(GROUPS):
            tails = jnp.concatenate([x_ref[n, 4 * g + j, :, MAIN:] for j in range(4)], axis=1)
            if tail_at(g) != LAST:
                keep(tail_at(g), tails)
        tiles = [tails[8 * u : 8 * (u + 1)] for u in range(LV // 8)]
        for d in range(MEMS):
            joined = pltpu.roll(tiles[0], CUT * (-d % MEMS), 1) if d else tiles[0]
            for u in range(1, LV // 8):
                shift = (u - d) % MEMS
                moved = pltpu.roll(tiles[u], CUT * shift, 1) if shift else tiles[u]
                joined = jnp.where(own_cut(u, joined.shape), moved, joined)
            packed[n, d, FULL * LV :] = joined
        for k in range(MEMS):
            share = packed.at[n, lax.rem(me_ref[0] + k, MEMS)]
            stores.append(pltpu.make_async_copy(share, o_refs[k].at[n], out_sems.at[n, k]))
            stores[-1].start()
    for copy in stores:
        copy.wait()


def spread(me, x):
    n = x.shape[0]
    return pl.pallas_call(
        spread_body,
        in_specs=[SMEM, HBM],
        out_specs=[HBM] * MEMS,
        out_shape=[pltpu.HBM((n, SHARE, MAIN), f32)] * MEMS,
        scratch_shapes=[
            pltpu.VMEM(x.shape, f32),
            pltpu.VMEM((n, MEMS, SHARE, MAIN), f32),
            dma((n,)),
            dma((n, MEMS)),
        ],
        compiler_params=params(16),
        name="spread",
    )(me, in_hbm(x))


def field_rows(k, f):
    return pl.ds(8 * k + f, TILES, stride=8 * K)


def share_rows(i, q, f):
    return pl.ds((i * TILES * Q + q) * 8 + f, TILES, stride=8 * Q)


def load_tile(ref, shared, k, f):
    if not shared:
        return ref[field_rows(k, f), :]
    if k != LAST:
        return ref[share_rows(k % MEMS, k // MEMS, f), :]
    value = ref[share_rows(0, FULL, f), :]
    for i in range(1, MEMS):
        value = jnp.where(own_cut(i, value.shape), ref[share_rows(i, FULL, f), :], value)
    return value


def filter_body(
    out_shared, x_ref, w_ref, gy_ref, ga_ref, gb_ref, gc_ref, o_hbm, ra_ref, rb_ref, rc_ref, last_ref, tails_ref, s_ref, o_ref, sems,
):
    wide = 2 * MAIN
    for f in range(FIELDS):
        last_ref[f] = load_tile(x_ref, not out_shared, LAST, f)

    def keep(s, j, lanes, value):
        for n, part in enumerate(split(value)):
            if s == 0:
                first = min(SPAN * (j + 1), FIRST) - SPAN * j
                ra_ref[n, SPAN * j : SPAN * j + first, lanes] = part[:first]
                if first < SPAN:
                    rb_ref[n, 0, :REST, lanes] = part[first:]
                    rb_ref[n, 1, :REST, lanes] = part[first:]
            elif s == 1:
                at = REST + SPAN * (j // 2)
                rb_ref[n, j % 2, at : at + SPAN, lanes] = part
            else:
                rc_ref[n, j, residue(s - 2), lanes] = part

    def y_filter(pair):
        parts = []
        for f in pair:
            for j in range(4):
                for g in range(GROUPS):
                    k = tail_at(g)
                    tail = last_ref[f] if k == LAST else load_tile(x_ref, not out_shared, k, f)
                    if j:
                        tail = pltpu.roll(tail, MAIN - TAIL * j, 1)
                    tail = tail[:, :TAIL]
                    main = load_tile(x_ref, not out_shared, main_at(4 * g + j), f)
                    parts.append(jnp.concatenate([main, tail], axis=1))
        hi, lo = split(jnp.concatenate(parts, axis=0))
        rows, cols = hi.shape[0], NS * NY
        both = dot(jnp.concatenate([hi, lo], axis=0), gy_ref[:, : cols + MAIN])
        y = both[:rows, :cols] + both[rows:, :cols]
        other = dot(hi, gy_ref[:, cols + MAIN :])
        y = y + jnp.concatenate([other, both[:rows, cols:]], axis=1)
        for i, f in enumerate(pair):
            lanes = slice(MAIN * f, MAIN * (f + 1))
            for j in range(4):
                at = SPAN * (4 * i + j)
                part = y[at : at + SPAN] * w_ref[f : f + 1, :]
                for s in range(NS):
                    keep(s, j, lanes, part[:, MAIN * s : MAIN * (s + 1)])
                tails_ref[f, j] = part[:, NS * MAIN :]

    def keep_tails():
        for q in range(FIELDS // 4):
            lanes = slice(MAIN * (FIELDS + q), MAIN * (FIELDS + q + 1))
            for j in range(4):
                for s in range(NS):
                    lane = TAIL * s
                    parts = [tails_ref[4 * q + i, j, :, lane : lane + TAIL] for i in range(4)]
                    keep(s, j, lanes, jnp.concatenate(parts, axis=1))

    def x_filter(lanes):
        def product(g, hi, lo):
            rows = g.shape[0] // 2
            both = dot(g, hi)
            return both[:rows] + both[rows:] + dot(g[:rows], lo)

        a = product(ga_ref[...], ra_ref[0, :, lanes], ra_ref[1, :, lanes])
        b = [product(gb_ref[p], rb_ref[0, p, :, lanes], rb_ref[1, p, :, lanes]) for p in range(2)]
        c = [product(gc_ref[j], rc_ref[0, j, :, lanes], rc_ref[1, j, :, lanes]) for j in range(4)]
        return [a[residue(j)] + b[j % 2][residue(j // 2)] + c[j] for j in range(4)]

    def x_main(pair):
        out = x_filter(slice(MAIN * pair[0], MAIN * pair[0] + wide))
        for i, f in enumerate(pair):
            for r in range(ROWS):
                g, j = r // 4, r % 4
                main = out[j][TILES * g : TILES * (g + 1), MAIN * i : MAIN * (i + 1)]
                at = TILES * (K * f + main_at(r))
                s_ref[at : at + TILES, :] = main

    def x_tails():
        out = x_filter(slice(MAIN * FIELDS, MAIN * FIELDS + wide))
        for f in range(FIELDS):
            lane = TAIL * f
            for g in range(GROUPS):
                rows = slice(TILES * g, TILES * (g + 1))
                parts = [out[j][rows, lane : lane + TAIL] for j in range(4)]
                at = TILES * (K * f + tail_at(g))
                s_ref[at : at + TILES, :] = jnp.concatenate(parts, axis=1)

    couples = [(f, f + 1) for f in range(0, FIELDS, 2)]
    y_filter(couples[0])
    y_filter(couples[1])
    x_main(couples[0])
    y_filter(couples[2])
    x_main(couples[1])
    y_filter(couples[3])
    keep_tails()
    x_main(couples[2])
    x_tails()
    x_main(couples[3])
    size = o_ref.shape[0] // MEMS
    stores = []
    for n in range(MEMS):
        if out_shared:
            cells = [(t, k, q) for q, k in enumerate([n, n + MEMS, n + 2 * MEMS, LAST]) for t in range(TILES)]
            spots = [(n * TILES + t) * Q + q for t, _, q in cells]
        else:
            cells = [(t, k, 0) for t in (2 * n, 2 * n + 1) for k in range(K)]
            spots = [K * t + k for t, k, _ in cells]
        for (t, k, _), at in zip(cells, spots):
            tile = s_ref[pl.ds(TILES * k + t, FIELDS, stride=TILES * K), :]
            o_ref[8 * at : 8 * (at + 1), :] = tile
        part = pl.ds(size * n, size)
        stores.append(pltpu.make_async_copy(o_ref.at[part], o_hbm.at[part], sems.at[n]))
        stores[-1].start()
    for copy in stores:
        copy.wait()


def filter_fields(x, w, filters, out_shared):
    rows = TILES * FIELDS * (MEMS * Q if out_shared else K)
    columns = FIELDS * NY
    return pl.pallas_call(
        lambda *refs: filter_body(out_shared, *refs),
        in_specs=[WHOLE] * (2 + len(filters)),
        out_specs=HBM,
        out_shape=pltpu.HBM((rows, MAIN), f32),
        scratch_shapes=[
            pltpu.VMEM((2, FIRST, columns), bf16),
            pltpu.VMEM((2, 2, PAIR, columns), bf16),
            pltpu.VMEM((2, 4, 2 * SPAN, columns), bf16),
            pltpu.VMEM((FIELDS, TILES, MAIN), f32),
            pltpu.VMEM((FIELDS, 4, SPAN, MAIN), f32),
            pltpu.VMEM((FIELDS * K * TILES, MAIN), f32),
            pltpu.VMEM((rows, MAIN), f32),
            dma((MEMS,)),
        ],
        compiler_params=params(36),
        name="filter_out" if out_shared else "filter_back",
    )(x, w, *filters)


def mix(v, x):
    hi, lo = split(x)
    return dot(v[0], hi) + dot(v[0], lo) + dot(v[1], hi)


def middle_body(scale, me_ref, x_ref, v_ref, *refs):
    e_refs, o_ref, wind_refs = list(refs[:MEMS]), refs[MEMS], refs[MEMS + 1 : 2 * MEMS + 1]
    cut_ref, wind_ref, ens_ref, sems = refs[2 * MEMS + 1 :]
    loads = [pltpu.make_async_copy(e_refs[k], ens_ref.at[k], sems.at[k]) for k in range(MEMS)]
    for copy in loads:
        copy.start()
    e_refs = [ens_ref.at[k] for k in range(MEMS)]
    v, vt = split(v_ref[...]), split(v_ref[...].T)
    me = me_ref[0]
    wind = [None, None]
    for k in range(MEMS):
        loads[k].wait()
        at = lax.rem(me + MEMS - k, MEMS)
        for m in range(2):
            tiles = [x_ref[at, m, :, q].reshape(LV, MAIN) for q in range(Q)]
            loc = mix(v, jnp.concatenate(tiles, axis=1))
            for c in range(2):
                joined = e_refs[k][m, c, FULL * LV :]
                for u in range(LV // 8):
                    moved = pltpu.roll(joined, CUT * lax.rem(me + MEMS - u, MEMS), 1)
                    cut_ref[k, m, c, 8 * u : 8 * (u + 1)] = moved
                tiles = [e_refs[k][m, c, LV * q : LV * (q + 1)] for q in range(FULL)]
                ens = jnp.concatenate(tiles + [cut_ref[k, m, c]], axis=1)
                wind[c] = ens * loc if wind[c] is None else wind[c] + ens * loc
    wind = [w * scale for w in wind]
    for c in range(2):
        for q in range(Q):
            tile = wind[c][:, MAIN * q : MAIN * (q + 1)]
            wind_ref[:, c, q] = tile.reshape(MEMS, LV // MEMS, MAIN)
    for k in range(MEMS):
        wind_refs[k][...] = wind_ref[lax.rem(me + k, MEMS)]
    for k in range(MEMS):
        at = lax.rem(me + MEMS - k, MEMS)
        for m in range(2):
            adj = None
            for c in range(2):
                tiles = [e_refs[k][m, c, LV * q : LV * (q + 1)] for q in range(FULL)]
                ens = jnp.concatenate(tiles + [cut_ref[k, m, c]], axis=1)
                adj = ens * wind[c] if adj is None else adj + ens * wind[c]
            back = mix(vt, adj * scale)
            for q in range(Q):
                tile = back[:, MAIN * q : MAIN * (q + 1)]
                o_ref[at, m, :, q] = tile.reshape(LV // 8, 8, MAIN)


def middle(me, x, v, ens, scale):
    return pl.pallas_call(
        lambda *refs: middle_body(scale, *refs),
        in_specs=[SMEM, WHOLE, WHOLE] + [HBM] * MEMS,
        out_specs=[WHOLE] * (1 + MEMS),
        out_shape=[jax.ShapeDtypeStruct((MEMS, 2, LV // 8, Q, 8, MAIN), f32)]
        + [jax.ShapeDtypeStruct((2, Q, LV // MEMS, MAIN), f32)] * MEMS,
        scratch_shapes=[
            pltpu.VMEM((MEMS, 2, 2, LV, MAIN), f32),
            pltpu.VMEM((MEMS, 2, Q, LV // MEMS, MAIN), f32),
            pltpu.VMEM((MEMS,) + ens[0].shape, f32),
            dma((MEMS,)),
        ],
        compiler_params=params(24),
        name="middle",
    )(me, x, v, *[in_hbm(e) for e in ens])


def swap(x, axes):
    return lax.all_to_all(x, axes, 0, 0, tiled=True)


ORDER = (2, 6, 4, 3, 5, 1, 7)


def shards(control, ens_perts, vert_corr, slab_wts, level_slab):
    members = control.shape[0]
    scale = 1.0 / math.sqrt(members * MEMS - 1)
    filters = constants()

    control = jnp.transpose(control, (0, 2, 1, 3))
    got = swap(pack(control).reshape(TILES, K, FIELDS, MAIN), "tile")

    me = lax.axis_index("mem").reshape(1)
    ens = jnp.transpose(ens_perts, (0, 1, 3, 2, 4)).reshape(4, ROWS, LV, NY)
    ens = list(spread(me, ens))
    for k in ORDER:
        ens[k] = lax.ppermute(ens[k], "mem", [(i, (i + k) % MEMS) for i in range(MEMS)])
    ens = [e.reshape(2, 2, SHARE, MAIN) for e in ens]

    level_wts = slab_wts[level_slab]
    first = FIELDS * (lax.axis_index("tile") % (LV // FIELDS))
    own = lax.dynamic_slice_in_dim(level_wts, first, FIELDS, 0)
    w = jnp.concatenate([jnp.repeat(own, MAIN, axis=1), jnp.repeat(own, TAIL, axis=1)], axis=1)

    smooth = filter_fields(got.reshape(TILES * K * FIELDS, MAIN), w, filters, True)
    got = swap(smooth.reshape(MEMS * TILES, Q, FIELDS, MAIN), ("mem", "tile"))
    got = got.reshape(MEMS, 2, LV // 8, Q, 8, MAIN)
    adj, *wind = middle(me, got, vert_corr, ens, scale)
    got = swap(adj.reshape(MEMS * TILES, Q, FIELDS, MAIN), ("mem", "tile"))
    smooth = filter_fields(got.reshape(MEMS * TILES * Q * FIELDS, MAIN), w, filters, False)
    smooth, wind = lax.optimization_barrier((smooth, wind))
    got = swap(smooth.reshape(TILES, K, FIELDS, MAIN), "tile")
    for k in range(1, MEMS):
        wind[k] = lax.ppermute(wind[k], "mem", [(i, (i + k) % MEMS) for i in range(MEMS)])
    wind = unpack_wind(me, wind)
    gradient = finish(got.reshape(2, LV // 8, K, 8, MAIN), control)
    return (jnp.transpose(wind, (0, 2, 1, 3)), jnp.transpose(gradient, (0, 2, 1, 3)))


def solution(mesh):
    return jax.shard_map(
        shards,
        mesh=mesh,
        in_specs=(P("mem", None, "tile", None), P("mem", None, None, "tile", None), P(), P(), P()),
        out_specs=(P(None, "mem", "tile", None), P("mem", None, "tile", None)),
        check_vma=False,
    )
```

profile of v0, /device:TPU:0, one launch (start us, length us, event | category | flops | bytes accessed | tf_op | source)
XLA Modules:
  0.0 192.9 jit_solution(5645331628397018300)
XLA Ops:
  0.6 2.7 %pack.1 = f32[2,8,25,8,128]{4,3,2,1,0:T(8,128)} custom-call(f32[2,20,64,160]{3,2,1,0:T(8,128)} %bitcast.25), custom_call_target="tpu_custom_call" | custom-call | tf_op jit(solution)/shard_map/pack/pallas_call | solution.py:156
  3.4 8.3 %all-to-all-start = ((f32[16,25,8,128]{3,2,1,0:T(8,128)}), f32[16,25,8,128]{3,2,1,0:T(8,128)S(1)}, u32[]{:S(2)}, u32[]{:S(2)}) async-start(f32[16,25,8,128]{3,2,1,0:T(8,128)} %bitcast.33), calls=%async_computation | async-start | bytes 3276800 | tf_op jit(solution)/shard_map/all_to_all | solution.py:527
  12.8 23.5 %all-to-all-done = f32[16,25,8,128]{3,2,1,0:T(8,128)S(1)} async-done(((f32[16,25,8,128]{3,2,1,0:T(8,128)}), f32[16,25,8,128]{3,2,1,0:T(8,128)S(1)}, u32[]{:S(2)}, u32[]{:S(2)}) %all-to-all-start) | async-done | bytes 1638432 | tf_op jit(solution)/shard_map/all_to_all | solution.py:527
  36.4 7.1 %filter_out.1 = f32[4096,128]{1,0:T(8,128)} custom-call(f32[3200,128]{1,0:T(8,128)S(1)} %bitcast.29, f32[8,640]{1,0:T(8,128)S(1)} %pad_maximum_fusion.refs_1_, bf16[160,1280]{1,0:T(8,128)(2,1)S(1)} %copy-done.1, bf16[640,256]{1,0:T(8,128)(2,1)S(1)} %copy-done.4, bf16[2,320,224]{2,1,0:T(8,128)(2,1)S(1)} %copy-done.3, bf16[4,160,160]{2,1,0:T(8,128)(2,1)S(1)} %copy-done.2), custom_call_target="tpu_custom_call" | custom-call | tf_op jit(solution)/shard_map/filter_out/pallas_call | solution.py:438
  43.5 6.9 %all-to-all-start.1 = ((f32[128,4,8,128]{3,2,1,0:T(8,128)}), f32[128,4,8,128]{3,2,1,0:T(8,128)S(1)}, u32[]{:S(2)}, u32[]{:S(2)}) async-start(f32[128,4,8,128]{3,2,1,0:T(8,128)} %bitcast.31), calls=%async_computation.1 | async-start | bytes 4194304 | tf_op jit(solution)/shard_map/all_to_all | solution.py:527
  50.4 4.0 %spread.1 = (f32[4,200,128]{2,1,0:T(8,128)}, f32[4,200,128]{2,1,0:T(8,128)}, f32[4,200,128]{2,1,0:T(8,128)}, f32[4,200,128]{2,1,0:T(8,128)}, f32[4,200,128]{2,1,...) custom-call(s32[1]{0:T(128)} %bitcast.me_ref.refs_0_, f32[4,20,64,160]{3,2,1,0:T(8,128)} %bitcast.34), custom_call_target="tpu_custom_call" | custom-call | tf_op jit(solution)/shard_map/spread/pallas_call | solution.py:283
  54.4 1.1 collective-permute-start.1
  55.5 2.0 %collective-permute-start.2 = (f32[4,200,128]{2,1,0:T(8,128)}, f32[4,200,128]{2,1,0:T(8,128)S(1)}, u32[]{:S(2)}, u32[]{:S(2)}) collective-permute-start(f32[4,200,128]{2,1,0:T(8,128)} %get-tuple-element.31), channel_id=1, source_target_pairs={{0,48},{16,64},{32,80},{48,96},{64,112},{80,0},{96,16},{112,32},{1... | collective-permute-start | bytes 1228808 | tf_op jit(solution)/shard_map/ppermute | solution.py:545
  57.4 2.1 %collective-permute-start.3 = (f32[4,200,128]{2,1,0:T(8,128)}, f32[4,200,128]{2,1,0:T(8,128)S(1)}, u32[]{:S(2)}, u32[]{:S(2)}) collective-permute-start(f32[4,200,128]{2,1,0:T(8,128)} %get-tuple-element.32), channel_id=1, source_target_pairs={{0,64},{16,80},{32,96},{48,112},{64,0},{80,16},{96,32},{112,48},{1... | collective-permute-start | bytes 1228808 | tf_op jit(solution)/shard_map/ppermute | solution.py:545
  59.5 1.6 collective-permute-start.4
  61.1 22.5 %collective-permute-done = f32[4,200,128]{2,1,0:T(8,128)S(1)} collective-permute-done((f32[4,200,128]{2,1,0:T(8,128)}, f32[4,200,128]{2,1,0:T(8,128)S(1)}, u32[]{:S(2)}, u32[]{:S(2)}) %collective-permute-start) | collective-permute-done | bytes 409632 | tf_op jit(solution)/shard_map/ppermute | solution.py:545
  83.7 0.7 collective-permute-start.5
  84.5 8.4 %collective-permute-start.6 = (f32[4,200,128]{2,1,0:T(8,128)}, f32[4,200,128]{2,1,0:T(8,128)}, u32[]{:S(2)}, u32[]{:S(2)}) collective-permute-start(f32[4,200,128]{2,1,0:T(8,128)} %get-tuple-element.35), channel_id=1, source_target_pairs={{0,112},{16,0},{32,16},{48,32},{64,48},{80,64},{96,80},{112,96},{1... | collective-permute-start | bytes 1228808 | tf_op jit(solution)/shard_map/ppermute | solution.py:545
  92.8 8.5 %collective-permute-done.2 = f32[4,200,128]{2,1,0:T(8,128)S(1)} collective-permute-done((f32[4,200,128]{2,1,0:T(8,128)}, f32[4,200,128]{2,1,0:T(8,128)S(1)}, u32[]{:S(2)}, u32[]{:S(2)}) %collective-permute-start.2) | collective-permute-done | bytes 409632 | tf_op jit(solution)/shard_map/ppermute | solution.py:545
  101.3 1.1 collective-permute-done.3
  102.5 4.7 %collective-permute-done.4 = f32[4,200,128]{2,1,0:T(8,128)S(1)} collective-permute-done((f32[4,200,128]{2,1,0:T(8,128)}, f32[4,200,128]{2,1,0:T(8,128)S(1)}, u32[]{:S(2)}, u32[]{:S(2)}) %collective-permute-start.4) | collective-permute-done | bytes 409632 | tf_op jit(solution)/shard_map/ppermute | solution.py:545
  107.2 0.7 copy-done.26
  108.0 0.8 copy-done.27
  108.7 4.2 %middle.1 = (f32[8,2,8,4,8,128]{5,4,3,2,1,0:T(8,128)S(1)}, f32[2,4,8,128]{3,2,1,0:T(8,128)S(1)}, f32[2,4,8,128]{3,2,1,0:T(8,128)S(1)}, f32[2,4,8,128]{3,2,1,0:T(...) custom-call(s32[1]{0:T(128)} %bitcast.me_ref.refs_0_, ...), custom_call_target="tpu_custom_call" | custom-call | tf_op jit(solution)/shard_map/middle/pallas_call | solution.py:509
  113.0 40.4 %all_to_all.20 = f32[128,4,8,128]{3,2,1,0:T(8,128)S(1)} all-to-all(f32[128,4,8,128]{3,2,1,0:T(8,128)S(1)} %bitcast.30), channel_id=1, replica_groups=mesh['mem'=8,'tile'=16] {'mem','tile'}, dimensions={0} | all-to-all | bytes 4194304 | tf_op jit(solution)/shard_map/all_to_all | solution.py:527
  153.4 7.8 %filter_back.1 = f32[3200,128]{1,0:T(8,128)} custom-call(f32[4096,128]{1,0:T(8,128)S(1)} %bitcast.28, f32[8,640]{1,0:T(8,128)S(1)} %pad_maximum_fusion.refs_1_, bf16[160,1280]{1,0:T(8,128)(2,1)S(1)} %copy-done.1, bf16[640,256]{1,0:T(8,128)(2,1)S(1)} %copy-done.4, bf16[2,320,224]{2,1,0:T(8,128)(2,1)S(1)} %copy-done.3, bf16[4,160,160]{2,1,0:T(8,128)(2,1)S(1)} %copy-done.2), custom_call_target="tpu_custom_call" | custom-call | tf_op jit(solution)/shard_map/filter_back/pallas_call | solution.py:438
  161.3 4.7 %all-to-all-start.3 = ((f32[16,25,8,128]{3,2,1,0:T(8,128)}), f32[16,25,8,128]{3,2,1,0:T(8,128)}, u32[]{:S(2)}, u32[]{:S(2)}) async-start(f32[16,25,8,128]{3,2,1,0:T(8,128)} %bitcast.32), calls=%async_computation.3 | async-start | bytes 3276800 | tf_op jit(solution)/shard_map/all_to_all | solution.py:527
  166.1 1.0 collective-permute-start.8
  167.1 1.3 collective-permute-start.9
  168.4 2.7 %collective-permute-start.10 = (f32[2,4,8,128]{3,2,1,0:T(8,128)S(1)}, f32[2,4,8,128]{3,2,1,0:T(8,128)S(1)}, u32[]{:S(2)}, u32[]{:S(2)}) collective-permute-start(f32[2,4,8,128]{3,2,1,0:T(8,128)S(1)} %copy-done.15), channel_id=1, source_target_pairs={{0,64},{16,80},{32,96},{48,112},{64,0},{80,16},{96,32},{112,48},{1... | collective-permute-start | bytes 98312 | tf_op jit(solution)/shard_map/ppermute | solution.py:562
  171.1 1.0 collective-permute-start.11
  172.1 0.9 collective-permute-start.12
  173.0 1.0 collective-permute-done.10.refs_4_
  174.5 1.8 collective-permute-done.12.refs_6_
  176.2 0.9 unpack_wind.1
  177.1 12.9 %all-to-all-done.3 = f32[16,25,8,128]{3,2,1,0:T(8,128)} async-done(((f32[16,25,8,128]{3,2,1,0:T(8,128)}), f32[16,25,8,128]{3,2,1,0:T(8,128)}, u32[]{:S(2)}, u32[]{:S(2)}) %all-to-all-start.3) | async-done | bytes 1638432 | tf_op jit(solution)/shard_map/all_to_all | solution.py:527
  190.0 2.7 %finish.1 = f32[2,20,64,160]{3,2,1,0:T(8,128)} custom-call(f32[2,8,25,8,128]{4,3,2,1,0:T(8,128)} %bitcast.21.y_hbm, f32[2,20,64,160]{3,2,1,0:T(8,128)S(1)} %bitcast.26), custom_call_target="tpu_custom_call" | custom-call | tf_op jit(solution)/shard_map/finish/pallas_call | solution.py:201
  (80 shorter events, 1.8 us)
Async XLA Ops:
  3.4 33.0 %copy-start.1 = (bf16[160,1280]{1,0:T(8,128)(2,1)S(1)}, bf16[160,1280]{1,0:T(8,128)(2,1)}, u32[]{:S(2)}) copy-start(bf16[160,1280]{1,0:T(8,128)(2,1)} %constant.36.clone.refs_2_) | copy-start | bytes 1228804
  3.4 33.0 %copy-start.2 = (bf16[4,160,160]{2,1,0:T(8,128)(2,1)S(1)}, bf16[4,160,160]{2,1,0:T(8,128)(2,1)}, u32[]{:S(2)}) copy-start(bf16[4,160,160]{2,1,0:T(8,128)(2,1)} %constant.39.clone.refs_5_) | copy-start | bytes 614404
  3.4 32.9 %copy-start.3 = (bf16[2,320,224]{2,1,0:T(8,128)(2,1)S(1)}, bf16[2,320,224]{2,1,0:T(8,128)(2,1)}, u32[]{:S(2)}) copy-start(bf16[2,320,224]{2,1,0:T(8,128)(2,1)} %constant.38.clone.refs_4_) | copy-start | bytes 860164
  3.4 32.9 %copy-start.4 = (bf16[640,256]{1,0:T(8,128)(2,1)S(1)}, bf16[640,256]{1,0:T(8,128)(2,1)}, u32[]{:S(2)}) copy-start(bf16[640,256]{1,0:T(8,128)(2,1)} %constant.37.clone.refs_3_) | copy-start | bytes 983044
  3.4 32.9 %all-to-all-start = ((f32[16,25,8,128]{3,2,1,0:T(8,128)}), f32[16,25,8,128]{3,2,1,0:T(8,128)S(1)}, u32[]{:S(2)}, u32[]{:S(2)}) async-start(f32[16,25,8,128]{3,2,1,0:T(8,128)} %bitcast.33), calls=%async_computation | async-start | bytes 3276800 | tf_op jit(solution)/shard_map/all_to_all | solution.py:527
  43.5 65.3 %all-to-all-start.1 = ((f32[128,4,8,128]{3,2,1,0:T(8,128)}), f32[128,4,8,128]{3,2,1,0:T(8,128)S(1)}, u32[]{:S(2)}, u32[]{:S(2)}) async-start(f32[128,4,8,128]{3,2,1,0:T(8,128)} %bitcast.31), calls=%async_computation.1 | async-start | bytes 4194304 | tf_op jit(solution)/shard_map/all_to_all | solution.py:527
  50.3 58.4 %copy-start.5 = (f32[64,64]{1,0:T(8,128)S(1)}, f32[64,64]{1,0:T(8,128)}, u32[]{:S(2)}) copy-start(f32[64,64]{1,0:T(8,128)} %refs_2_.3) | copy-start | bytes 49156
  54.4 29.3 %collective-permute-start = (f32[4,200,128]{2,1,0:T(8,128)}, f32[4,200,128]{2,1,0:T(8,128)S(1)}, u32[]{:S(2)}, u32[]{:S(2)}) collective-permute-start(f32[4,200,128]{2,1,0:T(8,128)} %get-tuple-element.29), channel_id=1, source_target_pairs={{0,16},{16,32},{32,48},{48,64},{64,80},{80,96},{96,112},{112,0},{1... | collective-permute-start | bytes 1228808 | tf_op jit(solution)/shard_map/ppermute | solution.py:545
  54.4 30.0 %collective-permute-start.1 = (f32[4,200,128]{2,1,0:T(8,128)}, f32[4,200,128]{2,1,0:T(8,128)S(1)}, u32[]{:S(2)}, u32[]{:S(2)}) collective-permute-start(f32[4,200,128]{2,1,0:T(8,128)} %get-tuple-element.30), channel_id=1, source_target_pairs={{0,32},{16,48},{32,64},{48,80},{64,96},{80,112},{96,0},{112,16},{1... | collective-permute-start | bytes 1228808 | tf_op jit(solution)/shard_map/ppermute | solution.py:545
  55.5 45.8 %collective-permute-start.2 = (f32[4,200,128]{2,1,0:T(8,128)}, f32[4,200,128]{2,1,0:T(8,128)S(1)}, u32[]{:S(2)}, u32[]{:S(2)}) collective-permute-start(f32[4,200,128]{2,1,0:T(8,128)} %get-tuple-element.31), channel_id=1, source_target_pairs={{0,48},{16,64},{32,80},{48,96},{64,112},{80,0},{96,16},{112,32},{1... | collective-permute-start | bytes 1228808 | tf_op jit(solution)/shard_map/ppermute | solution.py:545
  57.4 45.0 %collective-permute-start.3 = (f32[4,200,128]{2,1,0:T(8,128)}, f32[4,200,128]{2,1,0:T(8,128)S(1)}, u32[]{:S(2)}, u32[]{:S(2)}) collective-permute-start(f32[4,200,128]{2,1,0:T(8,128)} %get-tuple-element.32), channel_id=1, source_target_pairs={{0,64},{16,80},{32,96},{48,112},{64,0},{80,16},{96,32},{112,48},{1... | collective-permute-start | bytes 1228808 | tf_op jit(solution)/shard_map/ppermute | solution.py:545
  59.5 47.7 %collective-permute-start.4 = (f32[4,200,128]{2,1,0:T(8,128)}, f32[4,200,128]{2,1,0:T(8,128)S(1)}, u32[]{:S(2)}, u32[]{:S(2)}) collective-permute-start(f32[4,200,128]{2,1,0:T(8,128)} %get-tuple-element.33), channel_id=1, source_target_pairs={{0,80},{16,96},{32,112},{48,0},{64,16},{80,32},{96,48},{112,64},{1... | collective-permute-start | bytes 1228808 | tf_op jit(solution)/shard_map/ppermute | solution.py:545
  83.7 23.5 %copy-start.22 = (f32[4,200,128]{2,1,0:T(8,128)}, f32[4,200,128]{2,1,0:T(8,128)S(1)}, u32[]{:S(2)}) copy-start(f32[4,200,128]{2,1,0:T(8,128)S(1)} %collective-permute-done) | copy-start | bytes 1228804
  83.7 23.5 %collective-permute-start.5 = (f32[4,200,128]{2,1,0:T(8,128)}, f32[4,200,128]{2,1,0:T(8,128)S(1)}, u32[]{:S(2)}, u32[]{:S(2)}) collective-permute-start(f32[4,200,128]{2,1,0:T(8,128)} %get-tuple-element.34), channel_id=1, source_target_pairs={{0,96},{16,112},{32,0},{48,16},{64,32},{80,48},{96,64},{112,80},{1... | collective-permute-start | bytes 1228808 | tf_op jit(solution)/shard_map/ppermute | solution.py:545
  84.5 24.3 %collective-permute-start.6 = (f32[4,200,128]{2,1,0:T(8,128)}, f32[4,200,128]{2,1,0:T(8,128)}, u32[]{:S(2)}, u32[]{:S(2)}) collective-permute-start(f32[4,200,128]{2,1,0:T(8,128)} %get-tuple-element.35), channel_id=1, source_target_pairs={{0,112},{16,0},{32,16},{48,32},{64,48},{80,64},{96,80},{112,96},{1... | collective-permute-start | bytes 1228808 | tf_op jit(solution)/shard_map/ppermute | solution.py:545
  112.9 40.4 %copy-start.6 = (f32[2,4,8,128]{3,2,1,0:T(8,128)}, f32[2,4,8,128]{3,2,1,0:T(8,128)S(1)}, u32[]{:S(2)}) copy-start(f32[2,4,8,128]{3,2,1,0:T(8,128)S(1)} %get-tuple-element.45.refs_0_) | copy-start | bytes 98308
  113.0 40.4 %copy-start.8 = (f32[2,4,8,128]{3,2,1,0:T(8,128)}, f32[2,4,8,128]{3,2,1,0:T(8,128)S(1)}, u32[]{:S(2)}) copy-start(f32[2,4,8,128]{3,2,1,0:T(8,128)S(1)} %get-tuple-element.52) | copy-start | bytes 98308
  113.0 40.4 %copy-start.10 = (f32[2,4,8,128]{3,2,1,0:T(8,128)}, f32[2,4,8,128]{3,2,1,0:T(8,128)S(1)}, u32[]{:S(2)}) copy-start(f32[2,4,8,128]{3,2,1,0:T(8,128)S(1)} %get-tuple-element.51) | copy-start | bytes 98308
  113.0 40.4 %copy-start.12 = (f32[2,4,8,128]{3,2,1,0:T(8,128)}, f32[2,4,8,128]{3,2,1,0:T(8,128)S(1)}, u32[]{:S(2)}) copy-start(f32[2,4,8,128]{3,2,1,0:T(8,128)S(1)} %get-tuple-element.50) | copy-start | bytes 98308
  113.0 40.4 %copy-start.14 = (f32[2,4,8,128]{3,2,1,0:T(8,128)}, f32[2,4,8,128]{3,2,1,0:T(8,128)S(1)}, u32[]{:S(2)}) copy-start(f32[2,4,8,128]{3,2,1,0:T(8,128)S(1)} %get-tuple-element.49) | copy-start | bytes 98308
  113.0 40.4 %copy-start.16 = (f32[2,4,8,128]{3,2,1,0:T(8,128)}, f32[2,4,8,128]{3,2,1,0:T(8,128)S(1)}, u32[]{:S(2)}) copy-start(f32[2,4,8,128]{3,2,1,0:T(8,128)S(1)} %get-tuple-element.48) | copy-start | bytes 98308
  113.0 40.4 %copy-start.18 = (f32[2,4,8,128]{3,2,1,0:T(8,128)}, f32[2,4,8,128]{3,2,1,0:T(8,128)S(1)}, u32[]{:S(2)}) copy-start(f32[2,4,8,128]{3,2,1,0:T(8,128)S(1)} %get-tuple-element.47) | copy-start | bytes 98308
  113.0 40.4 %copy-start.20 = (f32[2,4,8,128]{3,2,1,0:T(8,128)}, f32[2,4,8,128]{3,2,1,0:T(8,128)S(1)}, u32[]{:S(2)}) copy-start(f32[2,4,8,128]{3,2,1,0:T(8,128)S(1)} %get-tuple-element.46) | copy-start | bytes 98308
  161.3 28.7 %copy-start = (f32[2,64,20,160]{3,1,2,0:T(8,128)S(1)}, f32[2,64,20,160]{3,1,2,0:T(8,128)}, u32[]{:S(2)}) copy-start(f32[2,64,20,160]{3,1,2,0:T(8,128)} %param.9) | copy-start | bytes 4915204
  161.3 28.7 %all-to-all-start.3 = ((f32[16,25,8,128]{3,2,1,0:T(8,128)}), f32[16,25,8,128]{3,2,1,0:T(8,128)}, u32[]{:S(2)}, u32[]{:S(2)}) async-start(f32[16,25,8,128]{3,2,1,0:T(8,128)} %bitcast.32), calls=%async_computation.3 | async-start | bytes 3276800 | tf_op jit(solution)/shard_map/all_to_all | solution.py:527
  166.0 6.1 %collective-permute-start.7 = (f32[2,4,8,128]{3,2,1,0:T(8,128)S(1)}, f32[2,4,8,128]{3,2,1,0:T(8,128)S(1)}, u32[]{:S(2)}, u32[]{:S(2)}) collective-permute-start(f32[2,4,8,128]{3,2,1,0:T(8,128)S(1)} %copy-done.21), channel_id=1, source_target_pairs={{0,16},{16,32},{32,48},{48,64},{64,80},{80,96},{96,112},{112,0},{1... | collective-permute-start | bytes 98312 | tf_op jit(solution)/shard_map/ppermute | solution.py:562
  166.1 6.9 %collective-permute-start.8 = (f32[2,4,8,128]{3,2,1,0:T(8,128)S(1)}, f32[2,4,8,128]{3,2,1,0:T(8,128)S(1)}, u32[]{:S(2)}, u32[]{:S(2)}) collective-permute-start(f32[2,4,8,128]{3,2,1,0:T(8,128)S(1)} %copy-done.19), channel_id=1, source_target_pairs={{0,32},{16,48},{32,64},{48,80},{64,96},{80,112},{96,0},{112,16},{1... | collective-permute-start | bytes 98312 | tf_op jit(solution)/shard_map/ppermute | solution.py:562
  167.1 6.0 %collective-permute-start.9 = (f32[2,4,8,128]{3,2,1,0:T(8,128)S(1)}, f32[2,4,8,128]{3,2,1,0:T(8,128)S(1)}, u32[]{:S(2)}, u32[]{:S(2)}) collective-permute-start(f32[2,4,8,128]{3,2,1,0:T(8,128)S(1)} %copy-done.17), channel_id=1, source_target_pairs={{0,48},{16,64},{32,80},{48,96},{64,112},{80,0},{96,16},{112,32},{1... | collective-permute-start | bytes 98312 | tf_op jit(solution)/shard_map/ppermute | solution.py:562
  168.4 5.6 %collective-permute-start.10 = (f32[2,4,8,128]{3,2,1,0:T(8,128)S(1)}, f32[2,4,8,128]{3,2,1,0:T(8,128)S(1)}, u32[]{:S(2)}, u32[]{:S(2)}) collective-permute-start(f32[2,4,8,128]{3,2,1,0:T(8,128)S(1)} %copy-done.15), channel_id=1, source_target_pairs={{0,64},{16,80},{32,96},{48,112},{64,0},{80,16},{96,32},{112,48},{1... | collective-permute-start | bytes 98312 | tf_op jit(solution)/shard_map/ppermute | solution.py:562
  171.1 3.3 %collective-permute-start.11 = (f32[2,4,8,128]{3,2,1,0:T(8,128)S(1)}, f32[2,4,8,128]{3,2,1,0:T(8,128)S(1)}, u32[]{:S(2)}, u32[]{:S(2)}) collective-permute-start(f32[2,4,8,128]{3,2,1,0:T(8,128)S(1)} %copy-done.13), channel_id=1, source_target_pairs={{0,80},{16,96},{32,112},{48,0},{64,16},{80,32},{96,48},{112,64},{1... | collective-permute-start | bytes 98312 | tf_op jit(solution)/shard_map/ppermute | solution.py:562
  172.1 4.2 %collective-permute-start.12 = (f32[2,4,8,128]{3,2,1,0:T(8,128)S(1)}, f32[2,4,8,128]{3,2,1,0:T(8,128)S(1)}, u32[]{:S(2)}, u32[]{:S(2)}) collective-permute-start(f32[2,4,8,128]{3,2,1,0:T(8,128)S(1)} %copy-done.11), channel_id=1, source_target_pairs={{0,96},{16,112},{32,0},{48,16},{64,32},{80,48},{96,64},{112,80},{1... | collective-permute-start | bytes 98312 | tf_op jit(solution)/shard_map/ppermute | solution.py:562
  173.0 3.2 %collective-permute-start.13 = (f32[2,4,8,128]{3,2,1,0:T(8,128)S(1)}, f32[2,4,8,128]{3,2,1,0:T(8,128)S(1)}, u32[]{:S(2)}, u32[]{:S(2)}) collective-permute-start(f32[2,4,8,128]{3,2,1,0:T(8,128)S(1)} %copy-done.9), channel_id=1, source_target_pairs={{0,112},{16,0},{32,16},{48,32},{64,48},{80,64},{96,80},{112,96},{1... | collective-permute-start | bytes 98312 | tf_op jit(solution)/shard_map/ppermute | solution.py:562
  (15 other events, 121.6 us)
where the time goes:
time: 193 us
  waiting for transfers between devices  76.7 us (40%)
  starting transfers between devices  42.6 us (22%)
  blocking collectives  40.4 us (21%)
  Pallas kernels  29.4 us (15%)
  local copies, waits for them, and re-layouts  2.62 us (1%)
    all_to_all x1, blocking collectives, swap(): return lax.all_to_all(x, axes, 0, 0, tiled=True)  40.4 us
    ppermute x7, waiting for transfers between devices, shards(): lax.ppermute(ens[k], 'mem', [(i, (i + k) % MEMS) for i in range(MEMS)])  37 us
    all_to_all x3, waiting for transfers between devices, swap(): return lax.all_to_all(x, axes, 0, 0, tiled=True)  36.5 us
    all_to_all x3, starting transfers between devices, swap(): return lax.all_to_all(x, axes, 0, 0, tiled=True)  19.9 us
    ppermute x7, starting transfers between devices, shards(): lax.ppermute(ens[k], 'mem', [(i, (i + k) % MEMS) for i in range(MEMS)])  15.8 us
    pallas_call x2, Pallas kernels, filter_fields(): pl.pallas_call(lambda *refs: filter_body(out_shared, *refs), in_specs=[WH...  14.8 us
    ppermute x7, starting transfers between devices, shards(): lax.ppermute(wind[k], 'mem', [(i, (i + k) % MEMS) for i in range(MEMS)])  6.94 us
    pallas_call x1, Pallas kernels, middle(): pl.pallas_call(lambda *refs: middle_body(scale, *refs), in_specs=[SMEM, W...  4.2 us
  transfers between devices with their start and end apart: 17, of which 10 were waited for; matrix products, arithmetic and copies ran while one was open for 1% of the time, Pallas kernels for 3%

commit v1 on v0

--- a/solution.py
+++ b/solution.py
@@ -124,6 +124,13 @@
 
 def tail_at(g):
     return 5 * g + 4
+
+
+def gather_row(tile, shift):
+    moved = pltpu.roll(pltpu.roll(tile, shift, 1), 0, 1, stride=CUT, stride_axis=0)
+    here = lax.broadcasted_iota(jnp.int32, tile.shape, 0)
+    lane = lax.broadcasted_iota(jnp.int32, tile.shape, 1) // CUT
+    return jnp.sum(jnp.where(lane == here, moved, 0.0), axis=0, keepdims=True)
 
 
 def own_cut(i, shape):
@@ -300,27 +307,32 @@
     return pl.ds(8 * k + f, TILES, stride=8 * K)
 
 
-def share_rows(i, q, f):
-    return pl.ds((i * TILES * Q + q) * 8 + f, TILES, stride=8 * Q)
+def share_rows(i, at):
+    return pl.ds(i * TILES * K + at, TILES, stride=K)
 
 
 def load_tile(ref, shared, k, f):
     if not shared:
         return ref[field_rows(k, f), :]
-    if k != LAST:
-        return ref[share_rows(k % MEMS, k // MEMS, f), :]
-    value = ref[share_rows(0, FULL, f), :]
-    for i in range(1, MEMS):
-        value = jnp.where(own_cut(i, value.shape), ref[share_rows(i, FULL, f), :], value)
-    return value
+    return ref[share_rows(k % MEMS, 8 * (k // MEMS) + f), :]
 
 
 def filter_body(
     out_shared, x_ref, w_ref, gy_ref, ga_ref, gb_ref, gc_ref, o_hbm, ra_ref, rb_ref, rc_ref, last_ref, tails_ref, s_ref, o_ref, sems,
 ):
     wide = 2 * MAIN
-    for f in range(FIELDS):
-        last_ref[f] = load_tile(x_ref, not out_shared, LAST, f)
+    if out_shared:
+        for f in range(FIELDS):
+            last_ref[f] = load_tile(x_ref, False, LAST, f)
+    else:
+        pieces = [x_ref[share_rows(i, 8 * FULL), :] for i in range(MEMS)]
+        for f in range(FIELDS):
+            last = None
+            for i in range(MEMS):
+                shift = (i - f) % MEMS
+                moved = pltpu.roll(pieces[i], CUT * shift, 1) if shift else pieces[i]
+                last = moved if i == 0 else jnp.where(own_cut(i, moved.shape), moved, last)
+            last_ref[f] = last
 
     def keep(s, j, lanes, value):
         for n, part in enumerate(split(value)):
@@ -399,7 +411,8 @@
             for g in range(GROUPS):
                 rows = slice(TILES * g, TILES * (g + 1))
                 parts = [out[j][rows, lane : lane + TAIL] for j in range(4)]
-                at = TILES * (K * f + tail_at(g))
+                back = out_shared and tail_at(g) == LAST
+                at = TILES * (K * (FIELDS - 1 - f if back else f) + tail_at(g))
                 s_ref[at : at + TILES, :] = jnp.concatenate(parts, axis=1)
 
     couples = [(f, f + 1) for f in range(0, FIELDS, 2)]
@@ -417,14 +430,15 @@
     stores = []
     for n in range(MEMS):
         if out_shared:
-            cells = [(t, k, q) for q, k in enumerate([n, n + MEMS, n + 2 * MEMS, LAST]) for t in range(TILES)]
-            spots = [(n * TILES + t) * Q + q for t, _, q in cells]
+            cells = [(t, n + MEMS * q, K * (n * TILES + t) + 8 * q) for q in range(FULL) for t in range(TILES)]
         else:
-            cells = [(t, k, 0) for t in (2 * n, 2 * n + 1) for k in range(K)]
-            spots = [K * t + k for t, k, _ in cells]
-        for (t, k, _), at in zip(cells, spots):
-            tile = s_ref[pl.ds(TILES * k + t, FIELDS, stride=TILES * K), :]
-            o_ref[8 * at : 8 * (at + 1), :] = tile
+            cells = [(t, k, 8 * (K * t + k)) for t in (2 * n, 2 * n + 1) for k in range(K)]
+        for t, k, at in cells:
+            o_ref[at : at + 8, :] = s_ref[pl.ds(TILES * k + t, FIELDS, stride=TILES * K), :]
+        for t in range(TILES if out_shared else 0):
+            tile = s_ref[pl.ds(TILES * LAST + t, FIELDS, stride=TILES * K), :]
+            at = K * (n * TILES + t) + 8 * FULL
+            o_ref[at : at + 1, :] = gather_row(tile, CUT * (-n % MEMS))
         part = pl.ds(size * n, size)
         stores.append(pltpu.make_async_copy(o_ref.at[part], o_hbm.at[part], sems.at[n]))
         stores[-1].start()
@@ -433,7 +447,7 @@
 
 
 def filter_fields(x, w, filters, out_shared):
-    rows = TILES * FIELDS * (MEMS * Q if out_shared else K)
+    rows = TILES * FIELDS * K
     columns = FIELDS * NY
     return pl.pallas_call(
         lambda *refs: filter_body(out_shared, *refs),
@@ -474,7 +488,16 @@
         loads[k].wait()
         at = lax.rem(me + MEMS - k, MEMS)
         for m in range(2):
-            tiles = [x_ref[at, m, :, q].reshape(LV, MAIN) for q in range(Q)]
+            tiles = []
+            for q in range(FULL):
+                parts = [x_ref[at, m, K * u + 8 * q : K * u + 8 * (q + 1), :] for u in range(LV // 8)]
+                tiles.append(jnp.concatenate(parts, axis=0))
+            parts = []
+            for u in range(LV // 8):
+                row = x_ref[at, m, K * u + 8 * FULL : K * (u + 1), :]
+                row = pltpu.roll(jnp.broadcast_to(row, (8, MAIN)), CUT * lax.rem(me + 1, MEMS), 1)
+                parts.append(pltpu.roll(row, 0, 1, stride=CUT, stride_axis=0))
+            tiles.append(jnp.concatenate(parts, axis=0))
             loc = mix(v, jnp.concatenate(tiles, axis=1))
             for c in range(2):
                 joined = e_refs[k][m, c, FULL * LV :]
@@ -500,9 +523,12 @@
                 ens = jnp.concatenate(tiles + [cut_ref[k, m, c]], axis=1)
                 adj = ens * wind[c] if adj is None else adj + ens * wind[c]
             back = mix(vt, adj * scale)
-            for q in range(Q):
-                tile = back[:, MAIN * q : MAIN * (q + 1)]
-                o_ref[at, m, :, q] = tile.reshape(LV // 8, 8, MAIN)
+            for u in range(LV // 8):
+                for q in range(FULL):
+                    tile = back[8 * u : 8 * (u + 1), MAIN * q : MAIN * (q + 1)]
+                    o_ref[at, m, K * u + 8 * q : K * u + 8 * (q + 1), :] = tile
+                row = gather_row(back[8 * u : 8 * (u + 1), MAIN * FULL :], CUT * lax.rem(MEMS - me, MEMS))
+                o_ref[at, m, K * u + 8 * FULL : K * (u + 1), :] = row
 
 
 def middle(me, x, v, ens, scale):
@@ -510,7 +536,7 @@
         lambda *refs: middle_body(scale, *refs),
         in_specs=[SMEM, WHOLE, WHOLE] + [HBM] * MEMS,
         out_specs=[WHOLE] * (1 + MEMS),
-        out_shape=[jax.ShapeDtypeStruct((MEMS, 2, LV // 8, Q, 8, MAIN), f32)]
+        out_shape=[jax.ShapeDtypeStruct((MEMS, 2, LV // 8 * K, MAIN), f32)]
         + [jax.ShapeDtypeStruct((2, Q, LV // MEMS, MAIN), f32)] * MEMS,
         scratch_shapes=[
             pltpu.VMEM((MEMS, 2, 2, LV, MAIN), f32),
@@ -551,11 +577,11 @@
     w = jnp.concatenate([jnp.repeat(own, MAIN, axis=1), jnp.repeat(own, TAIL, axis=1)], axis=1)
 
     smooth = filter_fields(got.reshape(TILES * K * FIELDS, MAIN), w, filters, True)
-    got = swap(smooth.reshape(MEMS * TILES, Q, FIELDS, MAIN), ("mem", "tile"))
-    got = got.reshape(MEMS, 2, LV // 8, Q, 8, MAIN)
+    got = swap(smooth.reshape(MEMS * TILES * K, 1, MAIN), ("mem", "tile"))
+    got = got.reshape(MEMS, 2, LV // 8 * K, MAIN)
     adj, *wind = middle(me, got, vert_corr, ens, scale)
-    got = swap(adj.reshape(MEMS * TILES, Q, FIELDS, MAIN), ("mem", "tile"))
-    smooth = filter_fields(got.reshape(MEMS * TILES * Q * FIELDS, MAIN), w, filters, False)
+    got = swap(adj.reshape(MEMS * TILES * K, 1, MAIN), ("mem", "tile"))
+    smooth = filter_fields(got.reshape(MEMS * TILES * K, MAIN), w, filters, False)
     smooth, wind = lax.optimization_barrier((smooth, wind))
     got = swap(smooth.reshape(TILES, K, FIELDS, MAIN), "tile")
     for k in range(1, MEMS):

time: 193 us -> 184 us (0.953)
  waiting for transfers between devices: 76.7 us -> 71.8 us
  blocking collectives: 40.4 us -> 35.8 us
    ppermute x7, waiting for transfers between devices: 37 us -> 32.1 us  [shards(): lax.ppermute(ens[k], 'mem', [(i, (i + k) % MEMS) for i in range(MEMS)])]
    all_to_all x1, blocking collectives: 40.4 us -> 35.8 us  [swap(): return lax.all_to_all(x, axes, 0, 0, tiled=True)]
where the time goes in v1:
time: 184 us; the launch traced here: 183 us
  waiting for transfers between devices  71.8 us (39%)
  starting transfers between devices  42.3 us (23%)
  blocking collectives  35.8 us (19%)
  Pallas kernels  29.9 us (16%)
  local copies, waits for them, and re-layouts  2.58 us (1%)
    all_to_all x3, waiting for transfers between devices, swap(): return lax.all_to_all(x, axes, 0, 0, tiled=True)  36.5 us
    all_to_all x1, blocking collectives, swap(): return lax.all_to_all(x, axes, 0, 0, tiled=True)  35.8 us
    ppermute x7, waiting for transfers between devices, shards(): lax.ppermute(ens[k], 'mem', [(i, (i + k) % MEMS) for i in range(MEMS)])  32.1 us
    all_to_all x3, starting transfers between devices, swap(): return lax.all_to_all(x, axes, 0, 0, tiled=True)  19.7 us
    ppermute x7, starting transfers between devices, shards(): lax.ppermute(ens[k], 'mem', [(i, (i + k) % MEMS) for i in range(MEMS)])  15.8 us
    pallas_call x2, Pallas kernels, filter_fields(): pl.pallas_call(lambda *refs: filter_body(out_shared, *refs), in_specs=[WH...  14.1 us
    ppermute x7, starting transfers between devices, shards(): lax.ppermute(wind[k], 'mem', [(i, (i + k) % MEMS) for i in range(MEMS)])  6.78 us
    pallas_call x1, Pallas kernels, middle(): pl.pallas_call(lambda *refs: middle_body(scale, *refs), in_specs=[SMEM, W...  5.43 us
  transfers between devices with their start and end apart: 17, of which 10 were waited for; matrix products, arithmetic and copies ran while one was open for 1% of the time, Pallas kernels for 3%

profile of v1, /device:TPU:0, one launch (start us, length us, event | category | flops | bytes accessed | tf_op | source)
XLA Modules:
  0.0 183.4 jit_solution(2198603030599676259)
XLA Ops:
  0.6 2.7 %pack.1 = f32[2,8,25,8,128]{4,3,2,1,0:T(8,128)} custom-call(f32[2,20,64,160]{3,2,1,0:T(8,128)} %bitcast.29), custom_call_target="tpu_custom_call" | custom-call | tf_op jit(solution)/shard_map/pack/pallas_call | solution.py:163
  3.4 8.3 %all-to-all-start = ((f32[16,25,8,128]{3,2,1,0:T(8,128)}), f32[16,25,8,128]{3,2,1,0:T(8,128)S(1)}, u32[]{:S(2)}, u32[]{:S(2)}) async-start(f32[16,25,8,128]{3,2,1,0:T(8,128)} %bitcast.35), calls=%async_computation | async-start | bytes 3276800 | tf_op jit(solution)/shard_map/all_to_all | solution.py:553
  12.8 23.5 %all-to-all-done = f32[16,25,8,128]{3,2,1,0:T(8,128)S(1)} async-done(((f32[16,25,8,128]{3,2,1,0:T(8,128)}), f32[16,25,8,128]{3,2,1,0:T(8,128)S(1)}, u32[]{:S(2)}, u32[]{:S(2)}) %all-to-all-start) | async-done | bytes 1638432 | tf_op jit(solution)/shard_map/all_to_all | solution.py:553
  36.4 7.1 %filter_out.1 = f32[3200,128]{1,0:T(8,128)} custom-call(f32[3200,128]{1,0:T(8,128)S(1)} %bitcast.32, f32[8,640]{1,0:T(8,128)S(1)} %pad_maximum_fusion.refs_1_, bf16[160,1280]{1,0:T(8,128)(2,1)S(1)} %copy-done.1, bf16[640,256]{1,0:T(8,128)(2,1)S(1)} %copy-done.4, bf16[2,320,224]{2,1,0:T(8,128)(2,1)S(1)} %copy-done.3, bf16[4,160,160]{2,1,0:T(8,128)(2,1)S(1)} %copy-done.2), custom_call_target="tpu_custom_call" | custom-call | tf_op jit(solution)/shard_map/filter_out/pallas_call | solution.py:452
  43.4 6.9 %all-to-all-start.1 = ((f32[3200,1,128]{2,1,0:T(1,128)}), f32[3200,1,128]{2,1,0:T(1,128)S(1)}, u32[]{:S(2)}, u32[]{:S(2)}) async-start(f32[3200,1,128]{2,1,0:T(1,128)} %bitcast.36), calls=%async_computation.1 | async-start | bytes 3276800 | tf_op jit(solution)/shard_map/all_to_all | solution.py:553
  50.3 4.0 %spread.1 = (f32[4,200,128]{2,1,0:T(8,128)}, f32[4,200,128]{2,1,0:T(8,128)}, f32[4,200,128]{2,1,0:T(8,128)}, f32[4,200,128]{2,1,0:T(8,128)}, f32[4,200,128]{2,1,...) custom-call(s32[1]{0:T(128)} %bitcast.me_ref.refs_0_, f32[4,20,64,160]{3,2,1,0:T(8,128)} %bitcast.38), custom_call_target="tpu_custom_call" | custom-call | tf_op jit(solution)/shard_map/spread/pallas_call | solution.py:290
  54.4 1.1 collective-permute-start.1
  55.5 2.0 %collective-permute-start.2 = (f32[4,200,128]{2,1,0:T(8,128)}, f32[4,200,128]{2,1,0:T(8,128)S(1)}, u32[]{:S(2)}, u32[]{:S(2)}) collective-permute-start(f32[4,200,128]{2,1,0:T(8,128)} %get-tuple-element.31), channel_id=1, source_target_pairs={{0,48},{16,64},{32,80},{48,96},{64,112},{80,0},{96,16},{112,32},{1... | collective-permute-start | bytes 1228808 | tf_op jit(solution)/shard_map/ppermute | solution.py:571
  57.4 2.1 %collective-permute-start.3 = (f32[4,200,128]{2,1,0:T(8,128)}, f32[4,200,128]{2,1,0:T(8,128)S(1)}, u32[]{:S(2)}, u32[]{:S(2)}) collective-permute-start(f32[4,200,128]{2,1,0:T(8,128)} %get-tuple-element.32), channel_id=1, source_target_pairs={{0,64},{16,80},{32,96},{48,112},{64,0},{80,16},{96,32},{112,48},{1... | collective-permute-start | bytes 1228808 | tf_op jit(solution)/shard_map/ppermute | solution.py:571
  59.5 1.6 collective-permute-start.4
  61.1 17.6 %collective-permute-done = f32[4,200,128]{2,1,0:T(8,128)S(1)} collective-permute-done((f32[4,200,128]{2,1,0:T(8,128)}, f32[4,200,128]{2,1,0:T(8,128)S(1)}, u32[]{:S(2)}, u32[]{:S(2)}) %collective-permute-start) | collective-permute-done | bytes 409632 | tf_op jit(solution)/shard_map/ppermute | solution.py:571
  78.7 0.7 collective-permute-start.5
  79.6 8.3 %collective-permute-start.6 = (f32[4,200,128]{2,1,0:T(8,128)}, f32[4,200,128]{2,1,0:T(8,128)}, u32[]{:S(2)}, u32[]{:S(2)}) collective-permute-start(f32[4,200,128]{2,1,0:T(8,128)} %get-tuple-element.35), channel_id=1, source_target_pairs={{0,112},{16,0},{32,16},{48,32},{64,48},{80,64},{96,80},{112,96},{1... | collective-permute-start | bytes 1228808 | tf_op jit(solution)/shard_map/ppermute | solution.py:571
  87.9 8.5 %collective-permute-done.2 = f32[4,200,128]{2,1,0:T(8,128)S(1)} collective-permute-done((f32[4,200,128]{2,1,0:T(8,128)}, f32[4,200,128]{2,1,0:T(8,128)S(1)}, u32[]{:S(2)}, u32[]{:S(2)}) %collective-permute-start.2) | collective-permute-done | bytes 409632 | tf_op jit(solution)/shard_map/ppermute | solution.py:571
  96.4 1.1 collective-permute-done.3
  97.6 4.7 %collective-permute-done.4 = f32[4,200,128]{2,1,0:T(8,128)S(1)} collective-permute-done((f32[4,200,128]{2,1,0:T(8,128)}, f32[4,200,128]{2,1,0:T(8,128)S(1)}, u32[]{:S(2)}, u32[]{:S(2)}) %collective-permute-start.4) | collective-permute-done | bytes 409632 | tf_op jit(solution)/shard_map/ppermute | solution.py:571
  102.3 0.7 copy-done.10
  103.0 0.8 copy-done.11
  103.8 5.4 %middle.1 = (f32[8,2,200,128]{3,2,1,0:T(8,128)S(1)}, f32[2,4,8,128]{3,2,1,0:T(8,128)S(1)}, f32[2,4,8,128]{3,2,1,0:T(8,128)S(1)}, f32[2,4,8,128]{3,2,1,0:T(8,128)...) custom-call(s32[1]{0:T(128)} %bitcast.me_ref.refs_0_, ...), custom_call_target="tpu_custom_call" | custom-call | tf_op jit(solution)/shard_map/middle/pallas_call | solution.py:535
  109.3 35.8 %all_to_all.20 = f32[3200,1,128]{2,1,0:T(1,128)S(1)} all-to-all(f32[3200,1,128]{2,1,0:T(1,128)S(1)} %bitcast.34), channel_id=1, replica_groups=mesh['mem'=8,'tile'=16] {'mem','tile'}, dimensions={0} | all-to-all | bytes 3276800 | tf_op jit(solution)/shard_map/all_to_all | solution.py:553
  145.0 7.0 %filter_back.1 = f32[3200,128]{1,0:T(8,128)} custom-call(f32[3200,128]{1,0:T(8,128)S(1)} %bitcast.33, f32[8,640]{1,0:T(8,128)S(1)} %pad_maximum_fusion.refs_1_, bf16[160,1280]{1,0:T(8,128)(2,1)S(1)} %copy-done.1, bf16[640,256]{1,0:T(8,128)(2,1)S(1)} %copy-done.4, bf16[2,320,224]{2,1,0:T(8,128)(2,1)S(1)} %copy-done.3, bf16[4,160,160]{2,1,0:T(8,128)(2,1)S(1)} %copy-done.2), custom_call_target="tpu_custom_call" | custom-call | tf_op jit(solution)/shard_map/filter_back/pallas_call | solution.py:452
  152.1 4.6 %all-to-all-start.3 = ((f32[16,25,8,128]{3,2,1,0:T(8,128)}), f32[16,25,8,128]{3,2,1,0:T(8,128)}, u32[]{:S(2)}, u32[]{:S(2)}) async-start(f32[16,25,8,128]{3,2,1,0:T(8,128)} %bitcast.37), calls=%async_computation.3 | async-start | bytes 3276800 | tf_op jit(solution)/shard_map/all_to_all | solution.py:553
  156.7 0.8 collective-permute-start.8
  157.5 1.4 collective-permute-start.9
  158.9 2.7 %collective-permute-start.10 = (f32[2,4,8,128]{3,2,1,0:T(8,128)S(1)}, f32[2,4,8,128]{3,2,1,0:T(8,128)S(1)}, u32[]{:S(2)}, u32[]{:S(2)}) collective-permute-start(f32[2,4,8,128]{3,2,1,0:T(8,128)S(1)} %get-tuple-element.49), channel_id=1, source_target_pairs={{0,64},{16,80},{32,96},{48,112},{64,0},{80,16},{96,32},{112,48},{1... | collective-permute-start | bytes 98312 | tf_op jit(solution)/shard_map/ppermute | solution.py:588
  161.6 0.9 collective-permute-start.11
  162.5 0.9 collective-permute-start.12
  163.5 1.0 collective-permute-done.10.refs_4_
  164.9 1.8 collective-permute-done.12.refs_6_
  166.7 0.9 unpack_wind.1
  167.6 12.9 %all-to-all-done.3 = f32[16,25,8,128]{3,2,1,0:T(8,128)} async-done(((f32[16,25,8,128]{3,2,1,0:T(8,128)}), f32[16,25,8,128]{3,2,1,0:T(8,128)}, u32[]{:S(2)}, u32[]{:S(2)}) %all-to-all-start.3) | async-done | bytes 1638432 | tf_op jit(solution)/shard_map/all_to_all | solution.py:553
  180.5 2.7 %finish.1 = f32[2,20,64,160]{3,2,1,0:T(8,128)} custom-call(f32[2,8,25,8,128]{4,3,2,1,0:T(8,128)} %bitcast.23.y_hbm, f32[2,20,64,160]{3,2,1,0:T(8,128)S(1)} %bitcast.30), custom_call_target="tpu_custom_call" | custom-call | tf_op jit(solution)/shard_map/finish/pallas_call | solution.py:208
  (48 shorter events, 1.7 us)
Async XLA Ops:
  3.4 8.4 %copy-start.12 = (f32[16,4]{0,1:T(4,128)S(1)}, f32[16,4]{0,1:T(4,128)}, u32[]{:S(2)}) copy-start(f32[16,4]{0,1:T(4,128)} %param.12) | copy-start | bytes 772
  3.4 8.5 %copy-start.13 = (s32[64]{0:T(128)S(1)}, s32[64]{0:T(128)}, u32[]{:S(2)}) copy-start(s32[64]{0:T(128)} %param.13) | copy-start | bytes 772
  3.4 33.0 %copy-start.1 = (bf16[160,1280]{1,0:T(8,128)(2,1)S(1)}, bf16[160,1280]{1,0:T(8,128)(2,1)}, u32[]{:S(2)}) copy-start(bf16[160,1280]{1,0:T(8,128)(2,1)} %constant.36.clone.refs_2_) | copy-start | bytes 1228804
  3.4 33.0 %copy-start.2 = (bf16[4,160,160]{2,1,0:T(8,128)(2,1)S(1)}, bf16[4,160,160]{2,1,0:T(8,128)(2,1)}, u32[]{:S(2)}) copy-start(bf16[4,160,160]{2,1,0:T(8,128)(2,1)} %constant.39.clone.refs_5_) | copy-start | bytes 614404
  3.4 32.9 %copy-start.3 = (bf16[2,320,224]{2,1,0:T(8,128)(2,1)S(1)}, bf16[2,320,224]{2,1,0:T(8,128)(2,1)}, u32[]{:S(2)}) copy-start(bf16[2,320,224]{2,1,0:T(8,128)(2,1)} %constant.38.clone.refs_4_) | copy-start | bytes 860164
  3.4 32.9 %copy-start.4 = (bf16[640,256]{1,0:T(8,128)(2,1)S(1)}, bf16[640,256]{1,0:T(8,128)(2,1)}, u32[]{:S(2)}) copy-start(bf16[640,256]{1,0:T(8,128)(2,1)} %constant.37.clone.refs_3_) | copy-start | bytes 983044
  3.4 32.9 %all-to-all-start = ((f32[16,25,8,128]{3,2,1,0:T(8,128)}), f32[16,25,8,128]{3,2,1,0:T(8,128)S(1)}, u32[]{:S(2)}, u32[]{:S(2)}) async-start(f32[16,25,8,128]{3,2,1,0:T(8,128)} %bitcast.35), calls=%async_computation | async-start | bytes 3276800 | tf_op jit(solution)/shard_map/all_to_all | solution.py:553
  43.4 60.4 %all-to-all-start.1 = ((f32[3200,1,128]{2,1,0:T(1,128)}), f32[3200,1,128]{2,1,0:T(1,128)S(1)}, u32[]{:S(2)}, u32[]{:S(2)}) async-start(f32[3200,1,128]{2,1,0:T(1,128)} %bitcast.36), calls=%async_computation.1 | async-start | bytes 3276800 | tf_op jit(solution)/shard_map/all_to_all | solution.py:553
  50.3 53.5 %copy-start.5 = (f32[64,64]{1,0:T(8,128)S(1)}, f32[64,64]{1,0:T(8,128)}, u32[]{:S(2)}) copy-start(f32[64,64]{1,0:T(8,128)} %refs_2_.3) | copy-start | bytes 49156
  54.4 24.3 %collective-permute-start = (f32[4,200,128]{2,1,0:T(8,128)}, f32[4,200,128]{2,1,0:T(8,128)S(1)}, u32[]{:S(2)}, u32[]{:S(2)}) collective-permute-start(f32[4,200,128]{2,1,0:T(8,128)} %get-tuple-element.29), channel_id=1, source_target_pairs={{0,16},{16,32},{32,48},{48,64},{64,80},{80,96},{96,112},{112,0},{1... | collective-permute-start | bytes 1228808 | tf_op jit(solution)/shard_map/ppermute | solution.py:571
  54.4 25.1 %collective-permute-start.1 = (f32[4,200,128]{2,1,0:T(8,128)}, f32[4,200,128]{2,1,0:T(8,128)S(1)}, u32[]{:S(2)}, u32[]{:S(2)}) collective-permute-start(f32[4,200,128]{2,1,0:T(8,128)} %get-tuple-element.30), channel_id=1, source_target_pairs={{0,32},{16,48},{32,64},{48,80},{64,96},{80,112},{96,0},{112,16},{1... | collective-permute-start | bytes 1228808 | tf_op jit(solution)/shard_map/ppermute | solution.py:571
  55.5 40.9 %collective-permute-start.2 = (f32[4,200,128]{2,1,0:T(8,128)}, f32[4,200,128]{2,1,0:T(8,128)S(1)}, u32[]{:S(2)}, u32[]{:S(2)}) collective-permute-start(f32[4,200,128]{2,1,0:T(8,128)} %get-tuple-element.31), channel_id=1, source_target_pairs={{0,48},{16,64},{32,80},{48,96},{64,112},{80,0},{96,16},{112,32},{1... | collective-permute-start | bytes 1228808 | tf_op jit(solution)/shard_map/ppermute | solution.py:571
  57.4 40.1 %collective-permute-start.3 = (f32[4,200,128]{2,1,0:T(8,128)}, f32[4,200,128]{2,1,0:T(8,128)S(1)}, u32[]{:S(2)}, u32[]{:S(2)}) collective-permute-start(f32[4,200,128]{2,1,0:T(8,128)} %get-tuple-element.32), channel_id=1, source_target_pairs={{0,64},{16,80},{32,96},{48,112},{64,0},{80,16},{96,32},{112,48},{1... | collective-permute-start | bytes 1228808 | tf_op jit(solution)/shard_map/ppermute | solution.py:571
  59.5 42.8 %collective-permute-start.4 = (f32[4,200,128]{2,1,0:T(8,128)}, f32[4,200,128]{2,1,0:T(8,128)S(1)}, u32[]{:S(2)}, u32[]{:S(2)}) collective-permute-start(f32[4,200,128]{2,1,0:T(8,128)} %get-tuple-element.33), channel_id=1, source_target_pairs={{0,80},{16,96},{32,112},{48,0},{64,16},{80,32},{96,48},{112,64},{1... | collective-permute-start | bytes 1228808 | tf_op jit(solution)/shard_map/ppermute | solution.py:571
  78.7 25.1 %copy-start.6 = (f32[4,200,128]{2,1,0:T(8,128)}, f32[4,200,128]{2,1,0:T(8,128)S(1)}, u32[]{:S(2)}) copy-start(f32[4,200,128]{2,1,0:T(8,128)S(1)} %collective-permute-done) | copy-start | bytes 1228804
  78.7 23.6 %collective-permute-start.5 = (f32[4,200,128]{2,1,0:T(8,128)}, f32[4,200,128]{2,1,0:T(8,128)S(1)}, u32[]{:S(2)}, u32[]{:S(2)}) collective-permute-start(f32[4,200,128]{2,1,0:T(8,128)} %get-tuple-element.34), channel_id=1, source_target_pairs={{0,96},{16,112},{32,0},{48,16},{64,32},{80,48},{96,64},{112,80},{1... | collective-permute-start | bytes 1228808 | tf_op jit(solution)/shard_map/ppermute | solution.py:571
  79.6 22.7 %copy-start.7 = (f32[4,200,128]{2,1,0:T(8,128)}, f32[4,200,128]{2,1,0:T(8,128)S(1)}, u32[]{:S(2)}) copy-start(f32[4,200,128]{2,1,0:T(8,128)S(1)} %collective-permute-done.1) | copy-start | bytes 1228804
  79.6 24.3 %collective-permute-start.6 = (f32[4,200,128]{2,1,0:T(8,128)}, f32[4,200,128]{2,1,0:T(8,128)}, u32[]{:S(2)}, u32[]{:S(2)}) collective-permute-start(f32[4,200,128]{2,1,0:T(8,128)} %get-tuple-element.35), channel_id=1, source_target_pairs={{0,112},{16,0},{32,16},{48,32},{64,48},{80,64},{96,80},{112,96},{1... | collective-permute-start | bytes 1228808 | tf_op jit(solution)/shard_map/ppermute | solution.py:571
  96.4 5.9 %copy-start.8 = (f32[4,200,128]{2,1,0:T(8,128)}, f32[4,200,128]{2,1,0:T(8,128)S(1)}, u32[]{:S(2)}) copy-start(f32[4,200,128]{2,1,0:T(8,128)S(1)} %collective-permute-done.2) | copy-start | bytes 1228804
  97.6 4.7 %copy-start.9 = (f32[4,200,128]{2,1,0:T(8,128)}, f32[4,200,128]{2,1,0:T(8,128)S(1)}, u32[]{:S(2)}) copy-start(f32[4,200,128]{2,1,0:T(8,128)S(1)} %collective-permute-done.3) | copy-start | bytes 1228804
  102.3 0.8 copy-start.10
  103.0 0.8 copy-start.11
  152.1 28.4 %copy-start = (f32[2,64,20,160]{3,1,2,0:T(8,128)S(1)}, f32[2,64,20,160]{3,1,2,0:T(8,128)}, u32[]{:S(2)}) copy-start(f32[2,64,20,160]{3,1,2,0:T(8,128)} %param.9) | copy-start | bytes 4915204
  152.1 28.4 %all-to-all-start.3 = ((f32[16,25,8,128]{3,2,1,0:T(8,128)}), f32[16,25,8,128]{3,2,1,0:T(8,128)}, u32[]{:S(2)}, u32[]{:S(2)}) async-start(f32[16,25,8,128]{3,2,1,0:T(8,128)} %bitcast.37), calls=%async_computation.3 | async-start | bytes 3276800 | tf_op jit(solution)/shard_map/all_to_all | solution.py:553
  156.6 5.9 %collective-permute-start.7 = (f32[2,4,8,128]{3,2,1,0:T(8,128)S(1)}, f32[2,4,8,128]{3,2,1,0:T(8,128)S(1)}, u32[]{:S(2)}, u32[]{:S(2)}) collective-permute-start(f32[2,4,8,128]{3,2,1,0:T(8,128)S(1)} %get-tuple-element.46), channel_id=1, source_target_pairs={{0,16},{16,32},{32,48},{48,64},{64,80},{80,96},{96,112},{112,0},{1... | collective-permute-start | bytes 98312 | tf_op jit(solution)/shard_map/ppermute | solution.py:588
  156.7 6.8 %collective-permute-start.8 = (f32[2,4,8,128]{3,2,1,0:T(8,128)S(1)}, f32[2,4,8,128]{3,2,1,0:T(8,128)S(1)}, u32[]{:S(2)}, u32[]{:S(2)}) collective-permute-start(f32[2,4,8,128]{3,2,1,0:T(8,128)S(1)} %get-tuple-element.47), channel_id=1, source_target_pairs={{0,32},{16,48},{32,64},{48,80},{64,96},{80,112},{96,0},{112,16},{1... | collective-permute-start | bytes 98312 | tf_op jit(solution)/shard_map/ppermute | solution.py:588
  157.5 5.9 %collective-permute-start.9 = (f32[2,4,8,128]{3,2,1,0:T(8,128)S(1)}, f32[2,4,8,128]{3,2,1,0:T(8,128)S(1)}, u32[]{:S(2)}, u32[]{:S(2)}) collective-permute-start(f32[2,4,8,128]{3,2,1,0:T(8,128)S(1)} %get-tuple-element.48), channel_id=1, source_target_pairs={{0,48},{16,64},{32,80},{48,96},{64,112},{80,0},{96,16},{112,32},{1... | collective-permute-start | bytes 98312 | tf_op jit(solution)/shard_map/ppermute | solution.py:588
  158.9 5.6 %collective-permute-start.10 = (f32[2,4,8,128]{3,2,1,0:T(8,128)S(1)}, f32[2,4,8,128]{3,2,1,0:T(8,128)S(1)}, u32[]{:S(2)}, u32[]{:S(2)}) collective-permute-start(f32[2,4,8,128]{3,2,1,0:T(8,128)S(1)} %get-tuple-element.49), channel_id=1, source_target_pairs={{0,64},{16,80},{32,96},{48,112},{64,0},{80,16},{96,32},{112,48},{1... | collective-permute-start | bytes 98312 | tf_op jit(solution)/shard_map/ppermute | solution.py:588
  161.6 3.3 %collective-permute-start.11 = (f32[2,4,8,128]{3,2,1,0:T(8,128)S(1)}, f32[2,4,8,128]{3,2,1,0:T(8,128)S(1)}, u32[]{:S(2)}, u32[]{:S(2)}) collective-permute-start(f32[2,4,8,128]{3,2,1,0:T(8,128)S(1)} %get-tuple-element.50), channel_id=1, source_target_pairs={{0,80},{16,96},{32,112},{48,0},{64,16},{80,32},{96,48},{112,64},{1... | collective-permute-start | bytes 98312 | tf_op jit(solution)/shard_map/ppermute | solution.py:588
  162.5 4.2 %collective-permute-start.12 = (f32[2,4,8,128]{3,2,1,0:T(8,128)S(1)}, f32[2,4,8,128]{3,2,1,0:T(8,128)S(1)}, u32[]{:S(2)}, u32[]{:S(2)}) collective-permute-start(f32[2,4,8,128]{3,2,1,0:T(8,128)S(1)} %get-tuple-element.51), channel_id=1, source_target_pairs={{0,96},{16,112},{32,0},{48,16},{64,32},{80,48},{96,64},{112,80},{1... | collective-permute-start | bytes 98312 | tf_op jit(solution)/shard_map/ppermute | solution.py:588
  163.4 3.3 %collective-permute-start.13 = (f32[2,4,8,128]{3,2,1,0:T(8,128)S(1)}, f32[2,4,8,128]{3,2,1,0:T(8,128)S(1)}, u32[]{:S(2)}, u32[]{:S(2)}) collective-permute-start(f32[2,4,8,128]{3,2,1,0:T(8,128)S(1)} %get-tuple-element.52), channel_id=1, source_target_pairs={{0,112},{16,0},{32,16},{48,32},{64,48},{80,64},{96,80},{112,96},{1... | collective-permute-start | bytes 98312 | tf_op jit(solution)/shard_map/ppermute | solution.py:588
